TPU v7x, 128 devices: a whole 4x4x4 slice. The times are simulated.
128 devices in a mesh: dp: 8 (over z, y_hi), fsdp: 16 (over y_lo, x, core).
Axes of the slice: x: 4, y: 4 (y_hi: 2, y_lo: 2; y = y_hi * 2 + y_lo), z: 4, core: 2. Of those that a mesh axis runs over, the one named last changes fastest.
Arguments:
- tokens: bfloat16 [16, 1024, 2048], P('dp', 'fsdp'), may hold values from -6 to 6
- w_qkv: bfloat16 [2048, 3072], P('fsdp', 'dp'), may hold values from -0.1875 to 0.1875
- w_out: bfloat16 [1024, 2048], P('fsdp', 'dp'), may hold values from -0.375 to 0.375
- ln_gain: float32 [2048], replicated, may hold values from 0.5 to 1.5
- ln_bias: float32 [2048], replicated, may hold values from -3 to 3
- kv_pool: bfloat16 [64, 128, 2048], P('fsdp'), may hold values from -300 to 300
- page_table: int32 [4, 16], replicated, may hold values from 0 to 63, as said below
- prefix_len: int32 [4], replicated, may hold values from 1 to 2048, as said below
- group_of: int32 [16], P('dp'), may hold values from 0 to 3, as said below
Outputs:
- hidden_out: bfloat16 [16, 1024, 2048], P('dp', 'fsdp')
- new_cache: bfloat16 [16, 1024, 2048], P('dp', 'fsdp')
Inputs may be any that keep to these rules, and one draw needn't show every extreme that they name: `page_table`: a permutation of the pool's slots. `prefix_len`: some group's prefix is exactly 2048 long. `group_of`: each group has 4 requests.
All inputs are finite; a program needn't handle non-finite values.
Results may differ from a plain program's by a relative error of at most 0.012.
The roundings to bfloat16 on the way count: a program that leaves them out, or rounds other values in their place, can miss the bound.
Values may be sent and summed in bfloat16 or wider, within the bound.
A program may use at most 128 MiB of HBM per device.

v0:
```python
import math
import jax
import jax.numpy as jnp
from jax import lax
from jax.sharding import PartitionSpec as P

HD = 128
neg_big = -1e30
ln_eps = 1e-06


def attend_rows(
    queries, row_req, row_pos, row_group, row_len, key_rows, value_rows, key_req, key_pos, key_group
):
    row_count = queries.shape[0]
    heads = queries.shape[1]
    head_dim = queries.shape[2]
    block_rows = min(512, row_count)
    inv_root = 1.0 / math.sqrt(head_dim)

    def one_block(first_row):
        q_block = lax.dynamic_slice_in_dim(queries, first_row, block_rows, 0)
        req_block = lax.dynamic_slice_in_dim(row_req, first_row, block_rows, 0)
        pos_block = lax.dynamic_slice_in_dim(row_pos, first_row, block_rows, 0)
        group_block = lax.dynamic_slice_in_dim(row_group, first_row, block_rows, 0)
        len_block = lax.dynamic_slice_in_dim(row_len, first_row, block_rows, 0)
        scores = (
            jnp.einsum("nhd,khd->nhk", q_block, key_rows, preferred_element_type=jnp.float32)
            * inv_root
        )
        from_prefix = (key_group[None, :] == group_block[:, None]) & (
            key_pos[None, :] < len_block[:, None]
        )
        from_new = (key_req[None, :] == req_block[:, None]) & (
            key_pos[None, :] <= pos_block[:, None]
        )
        is_live = jnp.where(key_req[None, :] < 0, from_prefix, from_new)
        scores = jnp.where(is_live[:, None, :], scores, neg_big)
        row_max = jnp.max(scores, axis=2)
        expo = jnp.where(is_live[:, None, :], jnp.exp(scores - row_max[:, :, None]), 0.0)
        row_total = jnp.sum(expo, axis=2)
        summed = jnp.einsum(
            "nhk,khd->nhd",
            expo.astype(jnp.bfloat16),
            value_rows,
            preferred_element_type=jnp.float32,
        )
        return (summed, row_max, row_total)

    starts = jnp.arange(row_count // block_rows, dtype=jnp.int32) * block_rows
    summed, row_max, row_total = lax.map(one_block, starts)
    return (
        summed.reshape(row_count, heads, head_dim),
        row_max.reshape(row_count, heads),
        row_total.reshape(row_count, heads),
    )


def body(tokens, w_qkv, w_out, ln_gain, ln_bias, kv_pool, page_table, prefix_len, group_of):
    req_count = tokens.shape[0]
    tok_count = tokens.shape[1]
    width = tokens.shape[2]
    owners = lax.axis_size("fsdp")
    owner_index = lax.axis_index("fsdp")
    inner = w_out.shape[0] * owners
    heads = inner // HD
    new_len = tok_count * owners
    flat_rows = tokens.reshape(req_count * tok_count, width)
    qkv_cols, out_cols = (
        lax.all_gather(w_qkv, "dp", axis=1, tiled=True),
        lax.all_gather(w_out, "dp", axis=1, tiled=True),
    )
    left_rows = flat_rows
    qkv_sum = jnp.dot(
        left_rows,
        lax.all_gather(qkv_cols, "fsdp", axis=0, tiled=True),
        preferred_element_type=jnp.float32,
    )
    qkv = qkv_sum.astype(jnp.bfloat16).reshape(req_count, tok_count, 3 * inner)
    own_queries = qkv[:, :, :inner]
    new_cache = qkv[:, :, inner:]
    own_keys = qkv[:, :, inner : 2 * inner]
    own_values = qkv[:, :, 2 * inner :]
    slot_count = kv_pool.shape[0]
    page_len = kv_pool.shape[1]
    group_count = page_table.shape[0]
    page_slots = page_table.shape[1]
    slot_ids = owner_index * slot_count + jnp.arange(slot_count, dtype=jnp.int32)
    matches = (page_table[:, :, None] == slot_ids[None, None, :]).astype(jnp.int32)
    slot_group = jnp.sum(
        matches * jnp.arange(group_count, dtype=jnp.int32)[:, None, None], axis=(0, 1)
    )
    slot_page = jnp.sum(
        matches * jnp.arange(page_slots, dtype=jnp.int32)[None, :, None], axis=(0, 1)
    )
    pool_pos = (
        slot_page[:, None] * page_len + jnp.arange(page_len, dtype=jnp.int32)[None, :]
    ).reshape(-1)
    pool_group = jnp.broadcast_to(slot_group[:, None], (slot_count, page_len)).reshape(-1)
    pool_req = jnp.full(pool_pos.shape, -1, jnp.int32)
    pool_keys = kv_pool[:, :, :inner].reshape(slot_count * page_len, heads, HD)
    pool_values = kv_pool[:, :, inner:].reshape(slot_count * page_len, heads, HD)
    member = (group_of[:, None] == jnp.arange(group_count, dtype=jnp.int32)[None, :]).astype(
        jnp.int32
    )
    request_len = jnp.sum(member * prefix_len[None, :], axis=1)

    def describe(row_positions):
        span_len = row_positions.shape[0]
        req_ids = jnp.broadcast_to(
            jnp.arange(req_count, dtype=jnp.int32)[:, None], (req_count, span_len)
        ).reshape(-1)
        pos_ids = jnp.broadcast_to(row_positions[None, :], (req_count, span_len)).reshape(-1)
        group_ids = jnp.broadcast_to(group_of[:, None], (req_count, span_len)).reshape(-1)
        len_ids = jnp.broadcast_to(request_len[:, None], (req_count, span_len)).reshape(-1)
        return (req_ids, pos_ids, group_ids, len_ids)

    all_positions = jnp.arange(new_len, dtype=jnp.int32)
    own_positions = owner_index * tok_count + jnp.arange(tok_count, dtype=jnp.int32)
    all_info = describe(all_positions)
    own_info = describe(own_positions)
    whole_q, whole_k, whole_v = (
        lax.all_gather(own_queries, "fsdp", axis=1, tiled=True),
        lax.all_gather(own_keys, "fsdp", axis=1, tiled=True),
        lax.all_gather(own_values, "fsdp", axis=1, tiled=True),
    )
    owner_sum, owner_max, owner_total = attend_rows(
        whole_q.reshape(req_count * new_len, heads, HD),
        all_info[0],
        all_info[1],
        all_info[2],
        all_info[3],
        pool_keys,
        pool_values,
        pool_req,
        pool_pos,
        pool_group,
    )
    owner_norm = (owner_sum / jnp.maximum(owner_total, 1.0)[:, :, None]).astype(jnp.bfloat16)
    part_norm = owner_norm.reshape(1, req_count, new_len, inner)
    part_max = owner_max.reshape(1, req_count, new_len, heads)
    part_total = owner_total.reshape(1, req_count, new_len, heads)
    got_norm = lax.all_to_all(part_norm, "fsdp", split_axis=2, concat_axis=0, tiled=True)
    got_max, got_total = (
        lax.all_to_all(part_max, "fsdp", split_axis=2, concat_axis=0, tiled=True),
        lax.all_to_all(part_total, "fsdp", split_axis=2, concat_axis=0, tiled=True),
    )
    local_sum, local_max, local_total = attend_rows(
        own_queries.reshape(req_count * tok_count, heads, HD),
        own_info[0],
        own_info[1],
        own_info[2],
        own_info[3],
        whole_k.reshape(req_count * new_len, heads, HD),
        whole_v.reshape(req_count * new_len, heads, HD),
        all_info[0],
        all_info[1],
        jnp.full(all_info[0].shape, -1, jnp.int32),
    )
    local_sum = local_sum.reshape(req_count, tok_count, heads, HD)
    local_max = local_max.reshape(req_count, tok_count, heads)
    local_total = local_total.reshape(req_count, tok_count, heads)
    overall = jnp.maximum(jnp.max(got_max, axis=0), local_max)
    factor = got_total * jnp.exp(got_max - overall[None])
    local_factor = jnp.exp(local_max - overall)
    part_count = got_norm.shape[0]
    normed_parts = got_norm.reshape(part_count, req_count, tok_count, heads, HD)
    numer = jnp.sum(normed_parts.astype(jnp.float32) * factor[..., None], axis=0)
    numer = numer + local_sum * local_factor[..., None]
    denom = jnp.sum(factor, axis=0) + local_total * local_factor
    attn = (numer / denom[..., None]).reshape(req_count * tok_count, inner).astype(jnp.bfloat16)
    left_rows = attn
    proj = jnp.dot(
        left_rows,
        lax.all_gather(out_cols, "fsdp", axis=0, tiled=True),
        preferred_element_type=jnp.float32,
    )
    mixed = flat_rows.astype(jnp.float32) + proj
    mean_row = jnp.mean(mixed, axis=1, keepdims=True)
    centred = mixed - mean_row
    var_row = jnp.mean(centred * centred, axis=1, keepdims=True)
    normed = centred * lax.rsqrt(var_row + ln_eps) * ln_gain[None, :] + ln_bias[None, :]
    hidden_out = normed.astype(jnp.bfloat16).reshape(req_count, tok_count, width)
    return (hidden_out, new_cache)


def solution(mesh):
    in_specs = (
        P("dp", "fsdp", None),
        P("fsdp", "dp"),
        P("fsdp", "dp"),
        P(),
        P(),
        P("fsdp", None, None),
        P(),
        P(),
        P("dp"),
    )
    out_specs = (P("dp", "fsdp", None), P("dp", "fsdp", None))
    return jax.shard_map(body, mesh=mesh, in_specs=in_specs, out_specs=out_specs, check_vma=False)
```

profile of v0, /device:TPU:3, one launch (start us, length us, event | category | flops | bytes accessed | tf_op | source)
XLA Modules:
  0.0 372.2 jit_solution(6619067220473818297)
XLA Ops:
  7.2 35.5 %all_gather.21 = bf16[128,3072]{1,0:T(8,128)(2,1)} all-gather(bf16[128,384]{1,0:T(8,128)(2,1)} %param.12), channel_id=1, replica_groups=mesh['dp'=8,'fsdp'=16] {'dp'}, dimensions={1}, use_global_device_ids=true | all-gather | bytes 884736 | tf_op jit(solution)/shard_map/all_gather | solution.py:70
  42.8 78.4 %all-gather.6.cloned.1.call-done = bf16[2048,3072]{1,0:T(8,128)(2,1)} async-done(((bf16[128,3072]{1,0:T(8,128)(2,1)}), bf16[2048,3072]{1,0:T(8,128)(2,1)}) %all-gather.6.cloned.1.call-update) | async-done | bytes 12582928 | tf_op jit(solution)/shard_map/all_gather | solution.py:76
  121.2 6.6 %convolution_convert_fusion = bf16[128,3072]{1,0:T(8,128)(2,1)S(1)} fusion(bf16[128,2048]{1,0:T(8,128)(2,1)} %bitcast.180, bf16[2048,3072]{1,0:T(8,128)(2,1)} %all-gather.6.cloned.1.call-done), kind=kOutput, calls=%fused_computation.42 | convolution fusion | flops 1611005952 | bytes 13893632 | tf_op jit(solution)/shard_map/dot_general | solution.py:74
  127.8 0.9 fusion.49
  128.8 0.7 all-gather.10.cloned.1.call-update
  130.1 31.3 %all_gather.26 = bf16[64,2048]{1,0:T(8,128)(2,1)} all-gather(bf16[64,256]{1,0:T(8,128)(2,1)S(1)} %copy-done.2), channel_id=1, replica_groups=mesh['dp'=8,'fsdp'=16] {'dp'}, dimensions={1}, use_global_device_ids=true | all-gather | bytes 294912 | tf_op jit(solution)/shard_map/all_gather | solution.py:71
  162.1 1.7 fusion.48
  165.2 2.3 all-gather.8.cloned.1.call-done
  167.5 5.2 %copy.131 = bf16[256,8,8,128]{3,2,1,0:T(8,128)(2,1)} copy(bf16[256,8,8,128]{3,1,2,0:T(8,128)(2,1)} %bitcast.169) | data formatting | bytes 8388608
  172.7 54.2 %while.4 = (s32[]{:T(128)}, f32[4,512,8,128]{3,2,1,0:T(8,128)}, f32[4,512,8]{1,2,0:T(8,128)S(1)}, f32[4,512,8]{1,2,0:T(8,128)S(1)}, s32[4]{0:T(128)S(1)}, /*inde...) while((s32[]{:T(128)}, f32[4,512,8,128]{3,2,1,0:T(8,128)}, ...), condition=%wide.region_6.7_spmd.clone, body=%wide.region_3.6_spmd.clone.sunk | while | flops 1101783552 | bytes 37900532 | solution.py:51
  172.7 0.6 dynamic_slice.42
  175.7 1.3 constant_dynamic-slice_fusion.2
  177.0 1.6 bitcast_reduce_fusion.3
  178.6 3.0 fusion.65
  181.6 2.6 copy_dynamic-update-slice_fusion.2
  184.3 2.0 fusion.66
  186.3 0.6 dynamic_slice.42
  189.3 1.3 constant_dynamic-slice_fusion.2
  190.6 1.6 bitcast_reduce_fusion.3
  192.3 3.0 fusion.65
  195.3 2.5 copy_dynamic-update-slice_fusion.2
  197.8 2.0 fusion.66
  199.8 0.6 dynamic_slice.42
  202.9 1.3 constant_dynamic-slice_fusion.2
  204.2 1.6 bitcast_reduce_fusion.3
  205.8 3.0 fusion.65
  208.8 2.6 copy_dynamic-update-slice_fusion.2
  211.4 2.0 fusion.66
  213.4 0.6 dynamic_slice.42
  216.4 1.3 constant_dynamic-slice_fusion.2
  217.7 1.6 bitcast_reduce_fusion.3
  219.3 3.0 fusion.65
  222.4 2.5 copy_dynamic-update-slice_fusion.2
  224.9 2.0 fusion.66
  227.0 0.5 copy.104
  227.5 2.2 reshape.384
  229.7 10.5 %all-to-all-start.2 = ((f32[16,1,1024]{2,1,0:T(1,128)}), f32[16,1,1024]{2,1,0:T(1,128)S(1)}, u32[]{:S(2)}, u32[]{:S(2)}) async-start(f32[16,1,1024]{2,1,0:T(1,128)} %reshape.384), calls=%async_computation.2 | async-start | bytes 131072 | tf_op jit(solution)/shard_map/all_to_all | solution.py:145
  240.2 0.5 copy.102
  240.7 2.2 reshape.386
  243.0 9.3 %reshape.377 = f32[1,2,1024,1024]{3,2,1,0:T(8,128)} reshape(f32[4,512,8,128]{3,2,1,0:T(8,128)} %get-tuple-element.136) | data formatting | bytes 16777216 | tf_op jit(solution)/shard_map/reshape | solution.py:53
  252.6 6.4 %div.34 = f32[2048,8,128]{2,1,0:T(8,128)} broadcast(f32[2048,8]{1,0:T(8,128)S(1)} %copy.100), dimensions={0,1} | broadcast | bytes 8454144 | tf_op jit(solution)/shard_map/div | solution.py:139
  258.9 9.3 %div.35 = f32[1,2,1024,1024]{3,2,1,0:T(8,128)} reshape(f32[2048,8,128]{2,1,0:T(8,128)} %div.34) | data formatting | bytes 16777216 | tf_op jit(solution)/shard_map/div | solution.py:139
  268.3 5.7 %all-to-all-start.1 = ((f32[16,1,1024]{2,1,0:T(1,128)}), f32[16,1,1024]{2,1,0:T(1,128)S(1)}, u32[]{:S(2)}, u32[]{:S(2)}) async-start(f32[16,1,1024]{2,1,0:T(1,128)} %reshape.386), calls=%async_computation.1 | async-start | bytes 131072 | tf_op jit(solution)/shard_map/all_to_all | solution.py:146
  274.0 7.8 %divide_convert_fusion = bf16[1,2,1024,1024]{3,2,1,0:T(8,128)(2,1)S(1)} fusion(f32[1,2,1024,1024]{3,2,1,0:T(8,128)} %reshape.377, f32[1,2,1024,1024]{3,2,1,0:T(8,128)} %div.35), kind=kLoop, calls=%fused_computation.30 | loop fusion | flops 4194304 | bytes 20971520 | tf_op jit(solution)/shard_map/convert_element_type | solution.py:139
  281.8 6.2 %copy.101 = bf16[1,2,1024,1024]{3,1,0,2:T(2,128)(2,1)} copy(bf16[1,2,1024,1024]{3,2,1,0:T(8,128)(2,1)S(1)} %divide_convert_fusion) | data formatting | bytes 8388608 | tf_op jit(solution)/shard_map/convert_element_type | solution.py:139
  288.1 6.1 %all-to-all-start = ((bf16[1,2,1024,1024]{3,1,0,2:T(2,128)(2,1)}), bf16[1,2,1024,1024]{3,1,0,2:T(2,128)(2,1)}, u32[]{:S(2)}, u32[]{:S(2)}) async-start(bf16[1,2,1024,1024]{3,1,0,2:T(2,128)(2,1)} %copy.101), calls=%async_computation | async-start | bytes 8388608 | tf_op jit(solution)/shard_map/all_to_all | solution.py:143
  294.2 1.7 and_select_fusion
  295.9 0.8 slice.27
  296.8 3.3 copy.136
  300.1 4.9 %fusion.22 = (f32[128,8]{0,1:T(8,128)S(1)}, f32[8,2048,128]{2,1,0:T(8,128)}) fusion(pred[128,2048]{0,1:T(8,128)(4,1)S(1)} %and_select_fusion, bf16[128,8,128]{2,1,0:T(8,128)(2,1)S(1)} %bitcast.189, bf16[2048,8,128]{2,1,0:T(8,128)(2,1)S(1)} %bitcast.170), kind=kOutput, calls=%fused_computation.31 | convolution fusion | flops 543161344 | bytes 13111296 | tf_op jit(solution)/shard_map/while/body/eval_jaxpr/nhd,khd->nhk/dot_general | solution.py:28
  305.1 4.5 %fusion.23 = f32[128,8]{0,1:T(8,128)S(1)} fusion(f32[8,2048,128]{2,1,0:T(8,128)} %get-tuple-element.280, f32[128,8]{0,1:T(8,128)S(1)} %get-tuple-element.279, pred[128,2048]{0,1:T(8,128)(4,1)S(1)} %and_select_fusion), kind=kLoop, calls=%fused_computation.32 | loop fusion | flops 10484736 | bytes 8658944 | tf_op jit(solution)/shard_map/while/body/eval_jaxpr/reduce_sum | solution.py:41
  309.6 3.3 copy.138
  312.9 5.7 %fusion.25 = f32[8,128,128]{2,1,0:T(8,128)S(1)} fusion(bf16[2048,8,128]{2,1,0:T(8,128)(2,1)S(1)} %bitcast.171, f32[8,2048,128]{2,1,0:T(8,128)} %get-tuple-element.280, f32[128,8]{0,1:T(8,128)S(1)} %get-tuple-element.279, pred[128,2048]{0,1:T(8,128)(4,1)S(1)} %and_select_fusion), kind=kOutput, calls=%fused_computation.34 | convolution fusion | flops 547356672 | bytes 13373440 | tf_op jit(solution)/shard_map/while/body/eval_jaxpr/nhk,khd->nhd/dot_general | solution.py:42
  319.3 0.8 reduce.2
  320.2 1.6 reshape.385
  322.2 0.8 reduce.3
  323.0 1.6 reshape.387
  325.4 0.6 copy.109
  326.0 4.6 %mul.121 = f32[16,2,64,8,128]{4,3,1,2,0:T(8,128)} broadcast(f32[16,2,64,8]{3,1,2,0:T(2,128)S(1)} %copy.109), dimensions={0,1,2,3} | broadcast | bytes 8454144 | tf_op jit(solution)/shard_map/mul | solution.py:168
  330.6 11.0 %mul.122 = f32[16,1,2,64,1024]{4,2,3,0,1:T(2,128)} reshape(f32[16,2,64,8,128]{4,3,1,2,0:T(8,128)} %mul.121) | data formatting | bytes 16777216 | tf_op jit(solution)/shard_map/mul | solution.py:168
  341.6 9.1 %all-to-all-done = bf16[1,2,1024,1024]{3,1,0,2:T(2,128)(2,1)} async-done(((bf16[1,2,1024,1024]{3,1,0,2:T(2,128)(2,1)}), bf16[1,2,1024,1024]{3,1,0,2:T(2,128)(2,1)}, u32[]{:S(2)}, u32[]{:S(2)}) %all-to-all-start) | async-done | bytes 4194336 | tf_op jit(solution)/shard_map/all_to_all | solution.py:143
  350.7 9.5 %fusion.21 = f32[2,64,1024]{2,0,1:T(2,128)S(1)} fusion(f32[16,1,2,64,1024]{4,2,3,0,1:T(2,128)} %mul.122, bf16[1,2,16,64,1024]{4,1,3,2,0:T(2,128)(2,1)} %bitcast.26), kind=kLoop, calls=%fused_computation.27 | loop fusion | flops 6160384 | bytes 13107200 | tf_op jit(solution)/shard_map/reduce_sum | solution.py:168
  361.1 3.0 fusion.50
  364.4 1.0 add_convert_fusion
  (104 shorter events, 8.6 us)
Async XLA Ops:
  7.2 114.0 %all-gather.6.cloned.1.call-start = ((), (), s32[]{:S(2)}) async-start(), calls=%async_computation.3 | async-start | bytes 13369344 | tf_op jit(solution)/shard_map/all_gather | solution.py:76
  42.8 124.7 %all-gather.8.cloned.1.call-start = ((), (), s32[]{:S(2)}) async-start(), calls=%async_computation.4 | async-start | bytes 4456448 | tf_op jit(solution)/shard_map/all_gather | solution.py:123
  121.2 8.9 %copy-start.2 = (bf16[64,256]{1,0:T(8,128)(2,1)S(1)}, bf16[64,256]{1,0:T(8,128)(2,1)}, u32[]{:S(2)}) copy-start(bf16[64,256]{1,0:T(8,128)(2,1)} %param.13) | copy-start | bytes 98308
  121.2 40.3 %copy-start.6 = (s32[2]{0:T(128)S(1)}, s32[2]{0:T(128)}, u32[]{:S(2)}) copy-start(s32[2]{0:T(128)} %param.19) | copy-start | bytes 28
  121.2 40.4 %copy-start.5 = (s32[4,16]{1,0:T(4,128)S(1)}, s32[4,16]{1,0:T(4,128)}, u32[]{:S(2)}) copy-start(s32[4,16]{1,0:T(4,128)} %param.17) | copy-start | bytes 772
  121.2 40.6 %copy-start.7 = (s32[4]{0:T(128)S(1)}, s32[4]{0:T(128)}, u32[]{:S(2)}) copy-start(s32[4]{0:T(128)} %param.18) | copy-start | bytes 52
  128.7 168.1 %all-gather.10.cloned.1.call-start = ((), (), s32[]{:S(2)}) async-start(), calls=%async_computation.5 | async-start | bytes 4456448 | tf_op jit(solution)/shard_map/all_gather | solution.py:124
  129.5 180.1 %all-gather.12.cloned.1.call-start = ((), (), s32[]{:S(2)}) async-start(), calls=%async_computation.6 | async-start | bytes 4456448 | tf_op jit(solution)/shard_map/all_gather | solution.py:125
  130.0 231.1 %all-gather.14.cloned.1.call-start = ((), (), s32[]{:S(2)}) async-start(), calls=%async_computation.7 | async-start | bytes 4456448 | tf_op jit(solution)/shard_map/all_gather | solution.py:175
  229.7 38.5 %all-to-all-start.2 = ((f32[16,1,1024]{2,1,0:T(1,128)}), f32[16,1,1024]{2,1,0:T(1,128)S(1)}, u32[]{:S(2)}, u32[]{:S(2)}) async-start(f32[16,1,1024]{2,1,0:T(1,128)} %reshape.384), calls=%async_computation.2 | async-start | bytes 131072 | tf_op jit(solution)/shard_map/all_to_all | solution.py:145
  268.3 19.8 %all-to-all-start.1 = ((f32[16,1,1024]{2,1,0:T(1,128)}), f32[16,1,1024]{2,1,0:T(1,128)S(1)}, u32[]{:S(2)}, u32[]{:S(2)}) async-start(f32[16,1,1024]{2,1,0:T(1,128)} %reshape.386), calls=%async_computation.1 | async-start | bytes 131072 | tf_op jit(solution)/shard_map/all_to_all | solution.py:146
  281.8 15.0 %copy-start.1 = (bf16[2,64,1024]{2,1,0:T(8,128)(2,1)S(1)}, bf16[2,64,1024]{2,1,0:T(8,128)(2,1)}, u32[]{:S(2)}) copy-start(bf16[2,64,1024]{2,1,0:T(8,128)(2,1)} %get-tuple-element.278) | copy-start | bytes 786436
  288.1 62.6 %all-to-all-start = ((bf16[1,2,1024,1024]{3,1,0,2:T(2,128)(2,1)}), bf16[1,2,1024,1024]{3,1,0,2:T(2,128)(2,1)}, u32[]{:S(2)}, u32[]{:S(2)}) async-start(bf16[1,2,1024,1024]{3,1,0,2:T(2,128)(2,1)} %copy.101), calls=%async_computation | async-start | bytes 8388608 | tf_op jit(solution)/shard_map/all_to_all | solution.py:143
  350.7 10.4 %copy-start = (bf16[2,64,2048]{2,1,0:T(8,128)(2,1)S(1)}, bf16[2,64,2048]{2,1,0:T(8,128)(2,1)}, u32[]{:S(2)}) copy-start(bf16[2,64,2048]{2,1,0:T(8,128)(2,1)} %param.11) | copy-start | bytes 1572868
  360.2 4.2 %copy-start.3 = (f32[2048]{0:T(1024)S(1)}, f32[2048]{0:T(1024)}, u32[]{:S(2)}) copy-start(f32[2048]{0:T(1024)} %param.15) | copy-start | bytes 24580
  360.2 4.2 %copy-start.4 = (f32[2048]{0:T(1024)S(1)}, f32[2048]{0:T(1024)}, u32[]{:S(2)}) copy-start(f32[2048]{0:T(1024)} %param.14) | copy-start | bytes 24580
Sparse Core Ops, SparseCore 0:
  42.9 78.2 all-gather.5
  128.9 38.5 all-gather.7
  169.1 37.3 all-gather.9
  208.6 37.4 all-gather.11
  247.7 37.9 all-gather.13
where the time goes:
time: 376 us; the launch traced here: 372 us
  local copies, waits for them, and re-layouts  94.5 us (25%)
  waiting for transfers between devices  91.1 us (24%)
  blocking collectives  66.9 us (18%)
  matrix products  38.6 us (10%)
  other arithmetic  36.6 us (10%)
  starting transfers between devices  22.5 us (6%)
  between operations  14.5 us (4%)
  loops' own time  7.53 us (2%)
    all_gather x1, waiting for transfers between devices, body(): lax.all_gather(qkv_cols, 'fsdp', axis=0, tiled=True)  78.4 us
    all_gather x1, blocking collectives, body(): lax.all_gather(w_qkv, 'dp', axis=1, tiled=True)  35.5 us
    all_gather x1, blocking collectives, body(): lax.all_gather(w_out, 'dp', axis=1, tiled=True)  31.3 us
    unnamed x32, local copies, waits for them, and re-layouts  20.5 us
    dot_general x5, matrix products, one_block(): jnp.einsum('nhk,khd->nhd', expo.astype(jnp.bfloat16), value_rows, preferr...  17.8 us
    div x2, local copies, waits for them, and re-layouts, body(): owner_sum / jnp.maximum(owner_total, 1.0)[:, :, None]  15.7 us
    mul x2, local copies, waits for them, and re-layouts, body(): normed_parts.astype(jnp.float32) * factor[..., None]  15.5 us
    reduce_sum x5, other arithmetic, one_block(): row_total = jnp.sum(expo, axis=2)  12.5 us
  transfers between devices with their start and end apart: 8, of which 3 were waited for; matrix products, arithmetic and copies ran while one was open for 42% of the time, Pallas kernels for 0%

commit v1 on v0

--- a/solution.py
+++ b/solution.py
@@ -3,6 +3,7 @@
 import jax.numpy as jnp
 from jax import lax
 from jax.sharding import PartitionSpec as P
+from jax.lax import all_to_all, axis_size
 
 HD = 128
 neg_big = -1e30
@@ -66,10 +67,16 @@
     heads = inner // HD
     new_len = tok_count * owners
     flat_rows = tokens.reshape(req_count * tok_count, width)
-    qkv_cols, out_cols = (
-        lax.all_gather(w_qkv, "dp", axis=1, tiled=True),
-        lax.all_gather(w_out, "dp", axis=1, tiled=True),
-    )
+
+    def bind_panels(axis_key, arr_in):
+        return jnp.concatenate(
+            all_to_all(
+                jnp.stack(tuple((arr_in for _ in range(axis_size(axis_key))))), axis_key, 0, 0
+            ),
+            1,
+        )
+
+    qkv_cols, out_cols = (lax.all_gather(w_qkv, "dp", axis=1, tiled=True), bind_panels("dp", w_out))
     left_rows = flat_rows
     qkv_sum = jnp.dot(
         left_rows,

time: 376 us -> 372 us (0.989)
  blocking collectives: 66.9 us -> 35.5 us
  waiting for transfers between devices: 91.1 us -> 114 us
    all_gather x1 -> x0, blocking collectives: 31.3 us -> none  [body(): lax.all_gather(w_out, 'dp', axis=1, tiled=True)]
    all_gather x1, waiting for transfers between devices: 2.29 us -> 21.3 us  [body(): lax.all_gather(own_queries, 'fsdp', axis=1, tiled=True)]
    all_to_all x0 -> x1, starting transfers between devices: none -> 6.59 us  [bind_panels(): all_to_all(jnp.stack(tuple((arr_in for _ in range(axis_size(axis_key)))))...]
    all_to_all x1, starting transfers between devices: 10.5 us -> 5.27 us  [body(): lax.all_to_all(part_max, 'fsdp', split_axis=2, concat_axis=0, tiled=True)]
  transfers between devices with their start and end apart: 8 -> 9, of which waited for: 3 -> 4; matrix products, arithmetic and copies ran while one was open for 42% -> 43% of each run, Pallas kernels for 0% -> 0%
where the time goes in v1:
time: 372 us; the launch traced here: 367 us
  waiting for transfers between devices  114 us (31%)
  local copies, waits for them, and re-layouts  96.1 us (26%)
  matrix products  38.7 us (10%)
  other arithmetic  36.7 us (10%)
  blocking collectives  35.5 us (10%)
  starting transfers between devices  24.1 us (6%)
  between operations  14.5 us (4%)
  loops' own time  7.99 us (2%)
    all_gather x1, waiting for transfers between devices, body(): lax.all_gather(qkv_cols, 'fsdp', axis=0, tiled=True)  78.4 us
    all_gather x1, blocking collectives, body(): lax.all_gather(w_qkv, 'dp', axis=1, tiled=True)  35.5 us
    all_gather x1, waiting for transfers between devices, body(): lax.all_gather(own_queries, 'fsdp', axis=1, tiled=True)  21.3 us
    unnamed x32, local copies, waits for them, and re-layouts  20.5 us
    dot_general x5, matrix products, one_block(): jnp.einsum('nhk,khd->nhd', expo.astype(jnp.bfloat16), value_rows, preferr...  17.8 us
    div x2, local copies, waits for them, and re-layouts, body(): owner_sum / jnp.maximum(owner_total, 1.0)[:, :, None]  15.7 us
    mul x2, local copies, waits for them, and re-layouts, body(): normed_parts.astype(jnp.float32) * factor[..., None]  15.5 us
    reduce_sum x5, other arithmetic, one_block(): row_total = jnp.sum(expo, axis=2)  12.5 us
  transfers between devices with their start and end apart: 9, of which 4 were waited for; matrix products, arithmetic and copies ran while one was open for 43% of the time, Pallas kernels for 0%

profile of v1, /device:TPU:3, one launch (start us, length us, event | category | flops | bytes accessed | tf_op | source)
XLA Modules:
  0.0 367.4 jit_solution(4965477434477831754)
XLA Ops:
  7.2 35.5 %all_gather.18 = bf16[128,3072]{1,0:T(8,128)(2,1)} all-gather(bf16[128,384]{1,0:T(8,128)(2,1)} %param.12), channel_id=1, replica_groups=mesh['dp'=8,'fsdp'=16] {'dp'}, dimensions={1}, use_global_device_ids=true | all-gather | bytes 884736 | tf_op jit(solution)/shard_map/all_gather | solution.py:79
  42.8 78.4 %all-gather.6.cloned.1.call-done = bf16[2048,3072]{1,0:T(8,128)(2,1)} async-done(((bf16[128,3072]{1,0:T(8,128)(2,1)}), bf16[2048,3072]{1,0:T(8,128)(2,1)}) %all-gather.6.cloned.1.call-update) | async-done | bytes 12582928 | tf_op jit(solution)/shard_map/all_gather | solution.py:83
  121.2 6.6 %convolution_convert_fusion = bf16[128,3072]{1,0:T(8,128)(2,1)S(1)} fusion(bf16[128,2048]{1,0:T(8,128)(2,1)} %bitcast.183, bf16[2048,3072]{1,0:T(8,128)(2,1)} %all-gather.6.cloned.1.call-done), kind=kOutput, calls=%fused_computation.42 | convolution fusion | flops 1611005952 | bytes 13893632 | tf_op jit(solution)/shard_map/dot_general | solution.py:81
  127.8 0.9 fusion.49
  128.8 0.7 all-gather.10.cloned.1.call-update
  130.1 0.7 stack.2
  130.8 6.6 %all-to-all-start.3 = ((bf16[8,64,256]{2,1,0:T(8,128)(2,1)}), bf16[8,64,256]{2,1,0:T(8,128)(2,1)S(1)}, u32[]{:S(2)}, u32[]{:S(2)}) async-start(bf16[8,64,256]{2,1,0:T(8,128)(2,1)} %stack.2), calls=%async_computation.3 | async-start | bytes 524288 | tf_op jit(solution)/shard_map/all_to_all | solution.py:73
  138.3 2.0 fusion.48
  141.7 3.7 %all-to-all-done.3 = bf16[8,64,256]{2,1,0:T(8,128)(2,1)S(1)} async-done(((bf16[8,64,256]{2,1,0:T(8,128)(2,1)}), bf16[8,64,256]{2,1,0:T(8,128)(2,1)S(1)}, u32[]{:S(2)}, u32[]{:S(2)}) %all-to-all-start.3) | async-done | bytes 262176 | tf_op jit(solution)/shard_map/all_to_all | solution.py:73
  145.4 0.7 copy.133
  146.2 21.3 %all-gather.8.cloned.1.call-done = bf16[2,1024,1024]{2,1,0:T(8,128)(2,1)} async-done(((bf16[2,64,1024]{2,1,0:T(8,128)(2,1)}), bf16[2,1024,1024]{2,1,0:T(8,128)(2,1)}) %all-gather.8.cloned.1.call-update) | async-done | bytes 4194320 | tf_op jit(solution)/shard_map/all_gather | solution.py:130
  167.5 5.2 %copy.136 = bf16[256,8,8,128]{3,2,1,0:T(8,128)(2,1)} copy(bf16[256,8,8,128]{3,1,2,0:T(8,128)(2,1)} %bitcast.172) | data formatting | bytes 8388608
  172.7 54.6 %while.4 = (s32[]{:T(128)}, f32[4,512,8,128]{3,2,1,0:T(8,128)}, f32[4,512,8]{1,2,0:T(8,128)S(1)}, f32[4,512,8]{1,2,0:T(8,128)S(1)}, s32[4]{0:T(128)S(1)}, /*inde...) while((s32[]{:T(128)}, f32[4,512,8,128]{3,2,1,0:T(8,128)}, ...), condition=%wide.region_6.7_spmd.clone, body=%wide.region_3.6_spmd.clone.sunk | while | flops 1101783552 | bytes 37900532 | solution.py:52
  172.7 0.6 dynamic_slice.42
  175.8 1.3 constant_dynamic-slice_fusion.2
  177.1 1.6 bitcast_reduce_fusion.3
  178.7 3.0 fusion.65
  181.7 2.6 copy_dynamic-update-slice_fusion.2
  184.3 2.0 fusion.66
  186.4 0.6 dynamic_slice.42
  189.5 1.3 constant_dynamic-slice_fusion.2
  190.8 1.6 bitcast_reduce_fusion.3
  192.4 3.0 fusion.65
  195.4 2.5 copy_dynamic-update-slice_fusion.2
  198.0 2.0 fusion.66
  200.0 0.6 dynamic_slice.42
  203.1 1.3 constant_dynamic-slice_fusion.2
  204.4 1.6 bitcast_reduce_fusion.3
  206.0 3.0 fusion.65
  209.1 2.5 copy_dynamic-update-slice_fusion.2
  211.6 2.0 fusion.66
  213.6 0.6 dynamic_slice.42
  216.8 1.3 constant_dynamic-slice_fusion.2
  218.1 1.6 bitcast_reduce_fusion.3
  219.7 3.0 fusion.65
  222.7 2.6 copy_dynamic-update-slice_fusion.2
  225.3 2.0 fusion.66
  227.8 2.2 reshape.394
  230.1 5.3 %all-to-all-start.2 = ((f32[16,1,1024]{2,1,0:T(1,128)}), f32[16,1,1024]{2,1,0:T(1,128)S(1)}, u32[]{:S(2)}, u32[]{:S(2)}) async-start(f32[16,1,1024]{2,1,0:T(1,128)} %reshape.394), calls=%async_computation.2 | async-start | bytes 131072 | tf_op jit(solution)/shard_map/all_to_all | solution.py:152
  235.9 2.2 reshape.396
  238.2 9.3 %reshape.385 = f32[1,2,1024,1024]{3,2,1,0:T(8,128)} reshape(f32[4,512,8,128]{3,2,1,0:T(8,128)} %get-tuple-element.136) | data formatting | bytes 16777216 | tf_op jit(solution)/shard_map/reshape | solution.py:54
  247.8 6.4 %div.34 = f32[2048,8,128]{2,1,0:T(8,128)} broadcast(f32[2048,8]{1,0:T(8,128)S(1)} %copy.103), dimensions={0,1} | broadcast | bytes 8454144 | tf_op jit(solution)/shard_map/div | solution.py:146
  254.2 9.3 %div.35 = f32[1,2,1024,1024]{3,2,1,0:T(8,128)} reshape(f32[2048,8,128]{2,1,0:T(8,128)} %div.34) | data formatting | bytes 16777216 | tf_op jit(solution)/shard_map/div | solution.py:146
  263.5 5.7 %all-to-all-start.1 = ((f32[16,1,1024]{2,1,0:T(1,128)}), f32[16,1,1024]{2,1,0:T(1,128)S(1)}, u32[]{:S(2)}, u32[]{:S(2)}) async-start(f32[16,1,1024]{2,1,0:T(1,128)} %reshape.396), calls=%async_computation.1 | async-start | bytes 131072 | tf_op jit(solution)/shard_map/all_to_all | solution.py:153
  269.2 7.8 %divide_convert_fusion = bf16[1,2,1024,1024]{3,2,1,0:T(8,128)(2,1)S(1)} fusion(f32[1,2,1024,1024]{3,2,1,0:T(8,128)} %reshape.385, f32[1,2,1024,1024]{3,2,1,0:T(8,128)} %div.35), kind=kLoop, calls=%fused_computation.30 | loop fusion | flops 4194304 | bytes 20971520 | tf_op jit(solution)/shard_map/convert_element_type | solution.py:146
  277.0 6.2 %copy.104 = bf16[1,2,1024,1024]{3,1,0,2:T(2,128)(2,1)} copy(bf16[1,2,1024,1024]{3,2,1,0:T(8,128)(2,1)S(1)} %divide_convert_fusion) | data formatting | bytes 8388608 | tf_op jit(solution)/shard_map/convert_element_type | solution.py:146
  283.3 6.0 %all-to-all-start = ((bf16[1,2,1024,1024]{3,1,0,2:T(2,128)(2,1)}), bf16[1,2,1024,1024]{3,1,0,2:T(2,128)(2,1)}, u32[]{:S(2)}, u32[]{:S(2)}) async-start(bf16[1,2,1024,1024]{3,1,0,2:T(2,128)(2,1)} %copy.104), calls=%async_computation | async-start | bytes 8388608 | tf_op jit(solution)/shard_map/all_to_all | solution.py:150
  289.3 1.7 and_select_fusion
  291.1 0.8 slice.27
  292.0 3.3 copy.141
  295.3 4.9 %fusion.22 = (f32[128,8]{0,1:T(8,128)S(1)}, f32[8,2048,128]{2,1,0:T(8,128)}) fusion(pred[128,2048]{0,1:T(8,128)(4,1)S(1)} %and_select_fusion, bf16[128,8,128]{2,1,0:T(8,128)(2,1)S(1)} %bitcast.194, bf16[2048,8,128]{2,1,0:T(8,128)(2,1)S(1)} %bitcast.173), kind=kOutput, calls=%fused_computation.31 | convolution fusion | flops 543161344 | bytes 13111296 | tf_op jit(solution)/shard_map/while/body/eval_jaxpr/nhd,khd->nhk/dot_general | solution.py:29
  300.2 4.5 %fusion.23 = f32[128,8]{0,1:T(8,128)S(1)} fusion(f32[8,2048,128]{2,1,0:T(8,128)} %get-tuple-element.280, f32[128,8]{0,1:T(8,128)S(1)} %get-tuple-element.279, pred[128,2048]{0,1:T(8,128)(4,1)S(1)} %and_select_fusion), kind=kLoop, calls=%fused_computation.32 | loop fusion | flops 10484736 | bytes 8658944 | tf_op jit(solution)/shard_map/while/body/eval_jaxpr/reduce_sum | solution.py:42
  304.8 3.3 copy.143
  308.0 5.7 %fusion.25 = f32[8,128,128]{2,1,0:T(8,128)S(1)} fusion(bf16[2048,8,128]{2,1,0:T(8,128)(2,1)S(1)} %bitcast.174, f32[8,2048,128]{2,1,0:T(8,128)} %get-tuple-element.280, f32[128,8]{0,1:T(8,128)S(1)} %get-tuple-element.279, pred[128,2048]{0,1:T(8,128)(4,1)S(1)} %and_select_fusion), kind=kOutput, calls=%fused_computation.34 | convolution fusion | flops 547356672 | bytes 13373440 | tf_op jit(solution)/shard_map/while/body/eval_jaxpr/nhk,khd->nhd/dot_general | solution.py:43
  314.5 0.8 reduce.2
  315.3 1.6 reshape.395
  317.4 0.8 reduce.3
  318.2 1.6 reshape.397
  321.2 4.5 %mul.121 = f32[16,2,64,8,128]{4,3,1,2,0:T(8,128)} broadcast(f32[16,2,64,8]{3,1,2,0:T(2,128)S(1)} %copy.112), dimensions={0,1,2,3} | broadcast | bytes 8454144 | tf_op jit(solution)/shard_map/mul | solution.py:175
  325.7 11.0 %mul.122 = f32[16,1,2,64,1024]{4,2,3,0,1:T(2,128)} reshape(f32[16,2,64,8,128]{4,3,1,2,0:T(8,128)} %mul.121) | data formatting | bytes 16777216 | tf_op jit(solution)/shard_map/mul | solution.py:175
  336.7 9.1 %all-to-all-done = bf16[1,2,1024,1024]{3,1,0,2:T(2,128)(2,1)} async-done(((bf16[1,2,1024,1024]{3,1,0,2:T(2,128)(2,1)}), bf16[1,2,1024,1024]{3,1,0,2:T(2,128)(2,1)}, u32[]{:S(2)}, u32[]{:S(2)}) %all-to-all-start) | async-done | bytes 4194336 | tf_op jit(solution)/shard_map/all_to_all | solution.py:150
  345.8 9.5 %fusion.21 = f32[2,64,1024]{2,0,1:T(2,128)S(1)} fusion(f32[16,1,2,64,1024]{4,2,3,0,1:T(2,128)} %mul.122, bf16[1,2,16,64,1024]{4,1,3,2,0:T(2,128)(2,1)} %bitcast.27), kind=kLoop, calls=%fused_computation.27 | loop fusion | flops 6160384 | bytes 13107200 | tf_op jit(solution)/shard_map/reduce_sum | solution.py:175
  356.3 3.0 fusion.50
  359.6 1.0 add_convert_fusion
  (107 shorter events, 10.5 us)
Async XLA Ops:
  7.2 114.0 %all-gather.6.cloned.1.call-start = ((), (), s32[]{:S(2)}) async-start(), calls=%async_computation.4 | async-start | bytes 13369344 | tf_op jit(solution)/shard_map/all_gather | solution.py:83
  42.8 124.7 %all-gather.8.cloned.1.call-start = ((), (), s32[]{:S(2)}) async-start(), calls=%async_computation.5 | async-start | bytes 4456448 | tf_op jit(solution)/shard_map/all_gather | solution.py:130
  121.2 8.8 %copy-start.2 = (bf16[64,256]{1,0:T(8,128)(2,1)S(1)}, bf16[64,256]{1,0:T(8,128)(2,1)}, u32[]{:S(2)}) copy-start(bf16[64,256]{1,0:T(8,128)(2,1)} %param.13) | copy-start | bytes 98308
  121.2 16.5 %copy-start.6 = (s32[2]{0:T(128)S(1)}, s32[2]{0:T(128)}, u32[]{:S(2)}) copy-start(s32[2]{0:T(128)} %param.19) | copy-start | bytes 28
  121.2 16.5 %copy-start.7 = (s32[4]{0:T(128)S(1)}, s32[4]{0:T(128)}, u32[]{:S(2)}) copy-start(s32[4]{0:T(128)} %param.18) | copy-start | bytes 52
  121.2 16.7 %copy-start.5 = (s32[4,16]{1,0:T(4,128)S(1)}, s32[4,16]{1,0:T(4,128)}, u32[]{:S(2)}) copy-start(s32[4,16]{1,0:T(4,128)} %param.17) | copy-start | bytes 772
  128.7 163.2 %all-gather.10.cloned.1.call-start = ((), (), s32[]{:S(2)}) async-start(), calls=%async_computation.6 | async-start | bytes 4456448 | tf_op jit(solution)/shard_map/all_gather | solution.py:131
  129.5 175.3 %all-gather.12.cloned.1.call-start = ((), (), s32[]{:S(2)}) async-start(), calls=%async_computation.7 | async-start | bytes 4456448 | tf_op jit(solution)/shard_map/all_gather | solution.py:132
  130.8 14.6 %all-to-all-start.3 = ((bf16[8,64,256]{2,1,0:T(8,128)(2,1)}), bf16[8,64,256]{2,1,0:T(8,128)(2,1)S(1)}, u32[]{:S(2)}, u32[]{:S(2)}) async-start(bf16[8,64,256]{2,1,0:T(8,128)(2,1)} %stack.2), calls=%async_computation.3 | async-start | bytes 524288 | tf_op jit(solution)/shard_map/all_to_all | solution.py:73
  137.4 218.9 %all-gather.14.cloned.1.call-start = ((), (), s32[]{:S(2)}) async-start(), calls=%async_computation.8 | async-start | bytes 4456448 | tf_op jit(solution)/shard_map/all_gather | solution.py:182
  230.1 33.4 %all-to-all-start.2 = ((f32[16,1,1024]{2,1,0:T(1,128)}), f32[16,1,1024]{2,1,0:T(1,128)S(1)}, u32[]{:S(2)}, u32[]{:S(2)}) async-start(f32[16,1,1024]{2,1,0:T(1,128)} %reshape.394), calls=%async_computation.2 | async-start | bytes 131072 | tf_op jit(solution)/shard_map/all_to_all | solution.py:152
  263.5 19.8 %all-to-all-start.1 = ((f32[16,1,1024]{2,1,0:T(1,128)}), f32[16,1,1024]{2,1,0:T(1,128)S(1)}, u32[]{:S(2)}, u32[]{:S(2)}) async-start(f32[16,1,1024]{2,1,0:T(1,128)} %reshape.396), calls=%async_computation.1 | async-start | bytes 131072 | tf_op jit(solution)/shard_map/all_to_all | solution.py:153
  277.0 14.9 %copy-start.1 = (bf16[2,64,1024]{2,1,0:T(8,128)(2,1)S(1)}, bf16[2,64,1024]{2,1,0:T(8,128)(2,1)}, u32[]{:S(2)}) copy-start(bf16[2,64,1024]{2,1,0:T(8,128)(2,1)} %get-tuple-element.278) | copy-start | bytes 786436
  283.3 62.5 %all-to-all-start = ((bf16[1,2,1024,1024]{3,1,0,2:T(2,128)(2,1)}), bf16[1,2,1024,1024]{3,1,0,2:T(2,128)(2,1)}, u32[]{:S(2)}, u32[]{:S(2)}) async-start(bf16[1,2,1024,1024]{3,1,0,2:T(2,128)(2,1)} %copy.104), calls=%async_computation | async-start | bytes 8388608 | tf_op jit(solution)/shard_map/all_to_all | solution.py:150
  345.8 10.4 %copy-start = (bf16[2,64,2048]{2,1,0:T(8,128)(2,1)S(1)}, bf16[2,64,2048]{2,1,0:T(8,128)(2,1)}, u32[]{:S(2)}) copy-start(bf16[2,64,2048]{2,1,0:T(8,128)(2,1)} %param.11) | copy-start | bytes 1572868
  355.4 4.2 %copy-start.3 = (f32[2048]{0:T(1024)S(1)}, f32[2048]{0:T(1024)}, u32[]{:S(2)}) copy-start(f32[2048]{0:T(1024)} %param.15) | copy-start | bytes 24580
  355.4 4.2 %copy-start.4 = (f32[2048]{0:T(1024)S(1)}, f32[2048]{0:T(1024)}, u32[]{:S(2)}) copy-start(f32[2048]{0:T(1024)} %param.14) | copy-start | bytes 24580
Sparse Core Ops, SparseCore 0:
  42.9 78.2 all-gather.5
  128.8 38.5 all-gather.7
  169.1 38.0 all-gather.9
  209.3 37.9 all-gather.11
  248.8 37.8 all-gather.13
